TPU v7x, 256 devices: a whole 4x4x8 slice. The times are simulated.
256 devices in a mesh: batch: 32 (over z, x), tensor: 8 (over y, core).
Axes of the slice: x: 4, y: 4, z: 8, core: 2. Of those that a mesh axis runs over, the one named last changes fastest.
Arguments:
- tokens: bfloat16 [8192, 4096], P(('batch', 'tensor')), may hold values from -6 to 6
- norm_gain: float32 [4096], replicated, may hold values from 0.1 to 1.9
- w_query: bfloat16 [4096, 4096], P(None, 'tensor'), may hold values from -0.09375 to 0.09375
- w_key: bfloat16 [4096, 1024], P(None, 'tensor'), may hold values from -0.25 to 0.25
- w_value: bfloat16 [4096, 1024], P(None, 'tensor'), may hold values from -0.09375 to 0.09375
- w_out: bfloat16 [4096, 4096], P('tensor'), may hold values from -0.25 to 0.25
- prefix_keys: bfloat16 [16384, 1024], P('batch', 'tensor'), may hold values from -6 to 6
- prefix_values: bfloat16 [16384, 1024], P('batch', 'tensor'), may hold values from -6 to 6
- cache_keys: bfloat16 [147456, 1024], P('batch', 'tensor'), may hold values from -160 to 160
- cache_values: bfloat16 [147456, 1024], P('batch', 'tensor'), may hold values from -6 to 6
- cache_lengths: int32 [128], replicated, may hold values from 128 to 2048, as said below
- prefix_used: int32 [128], P('batch'), may hold values from 4096 to 16384
- parents: int32 [128, 64], P('batch'), may hold values from 0 to 62, as said below
- accepted_index: int32 [128, 8], P('batch'), may hold values from 0 to 63, as said below
Outputs:
- mixed_output: bfloat16 [8192, 4096], P(('batch', 'tensor'))
- accepted_keys: bfloat16 [128, 8, 1024], P('batch', None, 'tensor')
- accepted_values: bfloat16 [128, 8, 1024], P('batch', None, 'tensor')
Inputs may be any that keep to these rules, and one draw needn't show every extreme that they name: `cache_lengths`: within each aligned group of 4 requests at most 2 have more than 256 cached tokens; in the first group exactly that many do, and some request has exactly 2048. parents[r, 0] = 0; for i >= 1, parents[r, i] lies between max(0, i - 8) and i - 1. `accepted_index`: each row lists 8 tree positions, each the parent of the next, ending at a position of 32 or more; where the root is reached the row repeats 0 at its front.
All inputs are finite; a program needn't handle non-finite values.
Results may differ from a plain program's by a relative error of at most 0.015.
The roundings to bfloat16 on the way count: a program that leaves them out, or rounds other values in their place, can miss the bound.
Values may be sent and summed in bfloat16 or wider, within the bound.
A program may use at most 192 MiB of HBM per device.

v0:
```python
import jax
import jax.numpy as jnp
from jax import lax
from jax.sharding import PartitionSpec as P

HD = 128


NEG_FILL = -1e30
HIGHEST = lax.Precision.HIGHEST


def rms_normed(tokens, norm_gain):
    values = tokens.astype(jnp.float32)
    factor = lax.rsqrt(jnp.mean(values * values, axis=-1, keepdims=True) + 1e-05)
    return (values * factor * norm_gain).astype(jnp.bfloat16)


def ancestor_table(parents):
    node_count = parents.shape[-1]
    column = jnp.arange(node_count, dtype=jnp.int32)
    linked = (parents[..., None] == column).astype(jnp.float32)
    itself = (column[:, None] == column[None, :]).astype(jnp.float32)
    ancestry = jnp.minimum(linked + itself, 1.0)
    for repeat in range(node_count.bit_length()):
        ancestry = jnp.minimum(
            jnp.einsum("rij,rjk->rik", ancestry, ancestry, precision=HIGHEST), 1.0
        )
    return ancestry


def rotate(values, positions):
    half_width = values.shape[-1] // 2
    frequency = 10000.0 ** (-jnp.arange(half_width, dtype=jnp.float32) / half_width)
    angles = positions.astype(jnp.float32)[:, None] * frequency[None, :]
    cosine = jnp.cos(angles)[:, None, :]
    sine_table = jnp.sin(angles)[:, None, :]
    first_half = values[..., :half_width]
    second_half = values[..., half_width:]
    return jnp.concatenate(
        [
            first_half * cosine - second_half * sine_table,
            second_half * cosine + first_half * sine_table,
        ],
        axis=-1,
    )


def absorb(carry, scores, visible, apply_values):
    running_max, running_sum, running_out = carry
    masked = jnp.where(visible, scores, NEG_FILL)
    new_max = jnp.maximum(running_max, jnp.max(masked, axis=-1))
    weights = jnp.where(visible, jnp.exp(masked - new_max[..., None]), 0.0)
    factor = jnp.exp(running_max - new_max)
    new_sum = running_sum * factor + jnp.sum(weights, axis=-1)
    new_out = running_out * factor[..., None] + apply_values(weights.astype(jnp.bfloat16))
    return (new_max, new_sum, new_out)


def combine(first_part, second_part):
    joint_max = jnp.maximum(first_part[0], second_part[0])
    first_factor = jnp.exp(first_part[0] - joint_max)
    second_factor = jnp.exp(second_part[0] - joint_max)
    joint_sum = first_part[1] * first_factor + second_part[1] * second_factor
    joint_out = first_part[2] * first_factor[..., None] + second_part[2] * second_factor[..., None]
    return (joint_max, joint_sum, joint_out)


def empty_partials(leading, head_size):
    return (
        jnp.full(leading, NEG_FILL, jnp.float32),
        jnp.zeros(leading, jnp.float32),
        jnp.zeros(leading + (head_size,), jnp.float32),
    )


def cache_partials(queries, all_keys, all_values, lower_slot, upper_slot, score_scale):
    capacity = all_keys.shape[0]
    block_size = min(512, capacity)
    kv_local = queries.shape[1]
    head_size = queries.shape[3]

    def one_request(request_items):
        request_query, lower_bound, upper_bound = request_items
        blocks = (upper_bound - lower_bound + block_size - 1) // block_size

        def block_step(block_index, carry):
            block_begin = lower_bound + block_index * block_size
            start = jnp.clip(block_begin, 0, capacity - block_size)
            block_keys = lax.dynamic_slice_in_dim(all_keys, start, block_size, 0).reshape(
                block_size, kv_local, head_size
            )
            block_values = lax.dynamic_slice_in_dim(all_values, start, block_size, 0).reshape(
                block_size, kv_local, head_size
            )
            slot_ids = start + jnp.arange(block_size, dtype=jnp.int32)
            visible = (slot_ids >= block_begin) & (
                slot_ids < jnp.minimum(upper_bound, block_begin + block_size)
            )
            scores = (
                jnp.einsum(
                    "hqd,khd->hqk", request_query, block_keys, preferred_element_type=jnp.float32
                )
                * score_scale
            )
            return absorb(
                carry,
                scores,
                visible[None, None, :],
                lambda rounded: jnp.einsum(
                    "hqk,khd->hqd", rounded, block_values, preferred_element_type=jnp.float32
                ),
            )

        start_carry = empty_partials(request_query.shape[:2], head_size)
        return lax.fori_loop(0, blocks, block_step, start_carry)

    return lax.map(one_request, (queries, lower_slot, upper_slot))


def body(
    tokens,
    norm_gain,
    w_query,
    w_key,
    w_value,
    w_out,
    prefix_keys,
    prefix_values,
    cache_keys,
    cache_values,
    cache_lengths,
    prefix_used,
    parents,
    accepted_index,
):
    req_count, tree_size = parents.shape
    head_size = HD
    query_cols = w_query.shape[1]
    key_cols = w_key.shape[1]
    kv_local = key_cols // head_size
    group_size = query_cols // key_cols
    query_rows = tree_size * group_size
    score_scale = head_size ** (-0.5)
    normed = rms_normed(tokens, norm_gain)
    piece = lax.all_gather(normed, "tensor", axis=0, tiled=True)
    projected = jnp.concatenate(
        [
            jnp.dot(piece, w_query, preferred_element_type=jnp.float32),
            jnp.dot(piece, w_key, preferred_element_type=jnp.float32),
            jnp.dot(piece, w_value, preferred_element_type=jnp.float32),
        ],
        axis=1,
    )
    group_index = lax.axis_index("batch")
    own_lengths = lax.dynamic_slice_in_dim(cache_lengths, group_index * req_count, req_count)
    ancestry = ancestor_table(parents)
    tree_depth = (jnp.sum(ancestry, axis=-1) - 1.0).astype(jnp.int32)
    position = ((prefix_used + own_lengths)[:, None] + tree_depth).reshape(req_count * tree_size)
    queries = rotate(
        projected[:, :query_cols].reshape(-1, kv_local * group_size, head_size), position
    ).astype(jnp.bfloat16)
    queries = queries.reshape(req_count, tree_size, kv_local, group_size, head_size).transpose(
        0, 2, 1, 3, 4
    )
    queries = queries.reshape(req_count, kv_local, query_rows, head_size)
    new_keys = rotate(
        projected[:, query_cols : query_cols + key_cols].reshape(-1, kv_local, head_size), position
    ).astype(jnp.bfloat16)
    new_keys = new_keys.reshape(req_count, tree_size, key_cols)
    new_values = (
        projected[:, query_cols + key_cols :]
        .astype(jnp.bfloat16)
        .reshape(req_count, tree_size, key_cols)
    )
    accepted_keys = jnp.take_along_axis(new_keys, accepted_index[:, :, None], axis=1)
    accepted_values = jnp.take_along_axis(new_values, accepted_index[:, :, None], axis=1)
    tree_keys = new_keys.reshape(req_count, tree_size, kv_local, head_size)
    tree_values = new_values.reshape(req_count, tree_size, kv_local, head_size)
    tree_scores = (
        jnp.einsum("rhqd,rkhd->rhqk", queries, tree_keys, preferred_element_type=jnp.float32)
        * score_scale
    )
    tree_visible = jnp.repeat(ancestry > 0.5, group_size, axis=1)[:, None]
    tree_part = absorb(
        empty_partials((req_count, kv_local, query_rows), head_size),
        tree_scores,
        tree_visible,
        lambda rounded: jnp.einsum(
            "rhqk,rkhd->rhqd", rounded, tree_values, preferred_element_type=jnp.float32
        ),
    )
    own_offsets = jnp.cumsum(own_lengths) - own_lengths
    cache_part = cache_partials(
        queries, cache_keys, cache_values, own_offsets, own_offsets + own_lengths, score_scale
    )
    local_part = combine(tree_part, cache_part)
    piece_keys = lax.all_gather(prefix_keys, "batch", axis=0, tiled=True)
    piece_values = lax.all_gather(prefix_values, "batch", axis=0, tiled=True)
    row_count = piece_keys.shape[0]
    shaped_keys = piece_keys.reshape(row_count, kv_local, head_size)
    shaped_values = piece_values.reshape(row_count, kv_local, head_size)
    slot_ids = jnp.arange(row_count, dtype=jnp.int32)
    visible = (slot_ids[None, :] < prefix_used[:, None])[:, None, None, :]
    scores = (
        jnp.einsum("rhqd,khd->rhqk", queries, shaped_keys, preferred_element_type=jnp.float32)
        * score_scale
    )
    folded = absorb(
        local_part,
        scores,
        visible,
        lambda rounded: jnp.einsum(
            "rhqk,khd->rhqd", rounded, shaped_values, preferred_element_type=jnp.float32
        ),
    )
    attended = (folded[2] / folded[1][..., None]).astype(jnp.bfloat16)
    attended = attended.reshape(req_count, kv_local, tree_size, group_size, head_size).transpose(
        0, 2, 1, 3, 4
    )
    attended = attended.reshape(req_count * tree_size, query_cols)
    mixed_rows = lax.psum_scatter(
        jnp.dot(attended, w_out, preferred_element_type=jnp.float32).astype(jnp.bfloat16),
        "tensor",
        scatter_dimension=0,
        tiled=True,
    )
    return (mixed_rows, accepted_keys, accepted_values)


def solution(mesh):
    in_specs = (
        P(("batch", "tensor"), None),
        P(),
        P(None, "tensor"),
        P(None, "tensor"),
        P(None, "tensor"),
        P("tensor", None),
        P("batch", "tensor"),
        P("batch", "tensor"),
        P("batch", "tensor"),
        P("batch", "tensor"),
        P(),
        P("batch"),
        P("batch", None),
        P("batch", None),
    )
    out_specs = (
        P(("batch", "tensor"), None),
        P("batch", None, "tensor"),
        P("batch", None, "tensor"),
    )
    return jax.shard_map(body, mesh=mesh, in_specs=in_specs, out_specs=out_specs, check_vma=False)
```

profile of v0, /device:TPU:33, one launch (start us, length us, event | category | flops | bytes accessed | tf_op | source)
XLA Modules:
  0.0 275.1 jit_solution(979624814477540230)
XLA Ops:
  7.2 1.2 fusion.52
  8.4 1.8 fusion.54
  10.3 0.7 all-gather.6.cloned.1.call-update
  11.0 0.7 all-gather.8.cloned.1.call-update
  11.8 0.8 iota_compare_fusion
  12.6 0.8 dynamic-slice_add_fusion
  13.6 0.7 bitcast_subtract_fusion
  14.3 1.0 convolution_minimum_fusion.6
  18.2 23.2 %all-gather.4.cloned.1.call-done = bf16[256,4096]{1,0:T(8,128)(2,1)} async-done(((bf16[32,4096]{1,0:T(8,128)(2,1)}), bf16[256,4096]{1,0:T(8,128)(2,1)}) %all-gather.4.cloned.1.call-update) | async-done | bytes 2097168 | tf_op jit(solution)/shard_map/all_gather | solution.py:146
  41.3 4.1 %fusion.85 = f32[256,512]{1,0:T(8,128)S(1)} fusion(bf16[256,4096]{1,0:T(8,128)(2,1)} %all-gather.4.cloned.1.call-done, bf16[4096,512]{1,0:T(8,128)(2,1)} %param.22), kind=kOutput, calls=%fused_computation.133 | convolution fusion | flops 1073741824 | bytes 6815744 | tf_op jit(solution)/shard_map/dot_general | solution.py:149
  46.1 0.9 pad_maximum_fusion.1
  47.0 32.6 %while.69 = (s32[]{:T(128)}, f32[4,1,256]{2,1,0:T(1,128)S(1)}, f32[4,1,256]{2,1,0:T(1,128)S(1)}, f32[4,1,256,128]{3,2,1,0:T(8,128)}, s32[4]{0:T(128)S(1)}, /*ind...) while((s32[]{:T(128)}, f32[4,1,256]{2,1,0:T(1,128)S(1)}, ...), condition=%wide.region_9.10_spmd, body=%wide.region_4.9_spmd.sunk | while | flops 68356632 | bytes 2712316 | solution.py:118
  49.7 0.9 dynamic-slice_bitcast_fusion.3
  50.6 4.0 %while.70 = (s32[]{:T(128)}, f32[1,256]{1,0:T(1,128)S(1)}, f32[1,256]{1,0:T(1,128)S(1)}, f32[1,256,128]{2,1,0:T(8,128)S(1)}, s32[]{:T(128)}, /*index=5*/s32[]{:T...) while((s32[]{:T(128)}, f32[1,256]{1,0:T(1,128)S(1)}, ...), condition=%wide.region_8.8_spmd, body=%wide.region_5.7_spmd.sunk | while | flops 68356616 | bytes 2181353 | solution.py:116
  51.9 1.2 fusion.117
  53.2 1.3 fusion.119
  57.8 0.9 dynamic-slice_bitcast_fusion.3
  58.7 4.0 %while.70 = (s32[]{:T(128)}, f32[1,256]{1,0:T(1,128)S(1)}, f32[1,256]{1,0:T(1,128)S(1)}, f32[1,256,128]{2,1,0:T(8,128)S(1)}, s32[]{:T(128)}, /*index=5*/s32[]{:T...) while((s32[]{:T(128)}, f32[1,256]{1,0:T(1,128)S(1)}, ...), condition=%wide.region_8.8_spmd, body=%wide.region_5.7_spmd.sunk | while | flops 68356616 | bytes 2181353 | solution.py:116
  60.0 1.2 fusion.117
  61.3 1.3 fusion.119
  62.7 0.7 bitcast_dynamic-update-slice_fusion.6
  65.9 0.9 dynamic-slice_bitcast_fusion.3
  66.8 4.0 %while.70 = (s32[]{:T(128)}, f32[1,256]{1,0:T(1,128)S(1)}, f32[1,256]{1,0:T(1,128)S(1)}, f32[1,256,128]{2,1,0:T(8,128)S(1)}, s32[]{:T(128)}, /*index=5*/s32[]{:T...) while((s32[]{:T(128)}, f32[1,256]{1,0:T(1,128)S(1)}, ...), condition=%wide.region_8.8_spmd, body=%wide.region_5.7_spmd.sunk | while | flops 68356616 | bytes 2181353 | solution.py:116
  68.0 1.2 fusion.117
  69.4 1.3 fusion.119
  74.0 0.9 dynamic-slice_bitcast_fusion.3
  74.8 4.0 %while.70 = (s32[]{:T(128)}, f32[1,256]{1,0:T(1,128)S(1)}, f32[1,256]{1,0:T(1,128)S(1)}, f32[1,256,128]{2,1,0:T(8,128)S(1)}, s32[]{:T(128)}, /*index=5*/s32[]{:T...) while((s32[]{:T(128)}, f32[1,256]{1,0:T(1,128)S(1)}, ...), condition=%wide.region_8.8_spmd, body=%wide.region_5.7_spmd.sunk | while | flops 68356616 | bytes 2181353 | solution.py:116
  76.1 1.2 fusion.117
  77.5 1.3 fusion.119
  79.6 0.8 convolution_bitcast_fusion.1
  80.4 0.9 fusion.68
  81.3 1.5 copy.30
  82.8 1.5 copy.29
  84.3 1.0 pad_maximum_fusion.2
  85.9 1.3 fusion.84
  87.3 0.7 copy-done.5
  88.0 2.5 convolution_convert_fusion.1
  90.6 31.1 %all-gather.6.cloned.1.call-done = bf16[16384,128]{1,0:T(8,128)(2,1)} async-done(((bf16[512,128]{1,0:T(8,128)(2,1)}), bf16[16384,128]{1,0:T(8,128)(2,1)}) %all-gather.6.cloned.1.call-update) | async-done | bytes 4194320 | tf_op jit(solution)/shard_map/all_gather | solution.py:198
  121.6 27.2 %fusion.17 = (f32[4,256]{1,0:T(4,128)S(1)}, f32[4,256,16384]{2,1,0:T(8,128)}) fusion(pred[4,16384]{1,0:T(4,128)(4,1)S(1)} %iota_compare_fusion, bf16[16384,128]{1,0:T(8,128)(2,1)} %all-gather.6.cloned.1.call-done, bf16[4,256,64]{2,1,0:T(8,128)(2,1)} %bitcast.194, bf16[4,256,64]{2,1,0:T(8,128)(2,1)S(1)} %bitcast.191), kind=kOutput, calls=%fused_computation.30 | convolution fusion | flops 4345822208 | bytes 71634944 | tf_op jit(solution)/shard_map/rhqd,khd->rhqk/dot_general | solution.py:206
  148.9 24.3 %fusion.18 = f32[4,256]{1,0:T(4,128)S(1)} fusion(f32[4,256,16384]{2,1,0:T(8,128)} %get-tuple-element.336, f32[4,256]{1,0:T(4,128)S(1)} %get-tuple-element.337, pred[4,16384]{1,0:T(4,128)(4,1)S(1)} %iota_compare_fusion), kind=kLoop, calls=%fused_computation.31 | loop fusion | flops 83885056 | bytes 67182592 | tf_op jit(solution)/shard_map/reduce_sum | solution.py:55
  173.3 1.0 fusion.45
  174.4 28.4 %all-gather.8.cloned.1.call-done = bf16[16384,128]{1,0:T(8,128)(2,1)} async-done(((bf16[512,128]{1,0:T(8,128)(2,1)}), bf16[16384,128]{1,0:T(8,128)(2,1)}) %all-gather.8.cloned.1.call-update) | async-done | bytes 4194320 | tf_op jit(solution)/shard_map/all_gather | solution.py:199
  202.8 25.9 %fusion.46 = bf16[4,1,256,128]{3,2,0,1:T(8,128)(2,1)S(1)} fusion(f32[4,1,256,128]{3,2,0,1:T(8,128)S(1)} %fusion.45, bf16[16384,128]{1,0:T(8,128)(2,1)} %all-gather.8.cloned.1.call-done, f32[4,256,16384]{2,1,0:T(8,128)} %get-tuple-element.336, f32[4,256]{1,0:T(4,128)S(1)} %get-tuple-element.337, pred[4,16384]{1,0:T(4,128)(4,1)S(1)} %iota_compare_fusion, ...), kind=kOutput, calls=%fused_computation.48 | convolution fusion | flops 4379246592 | bytes 72163328 | tf_op jit(solution)/shard_map/rhqk,khd->rhqd/dot_general | solution.py:213
  228.8 4.8 %convolution_convert_fusion = bf16[256,4096]{1,0:T(8,128)(2,1)} fusion(bf16[256,512]{1,0:T(8,128)(2,1)S(1)} %reshape_transpose_reshape.4, bf16[512,4096]{1,0:T(8,128)(2,1)} %param.25), kind=kOutput, calls=%fused_computation.36 | convolution fusion | flops 1074790400 | bytes 6553600 | tf_op jit(solution)/shard_map/dot_general | solution.py:223
  233.8 0.7 gather_fusion.1
  234.5 0.7 gather_fusion
  235.1 0.7 bitcast_select_fusion.1
  235.8 32.8 %reduce-scatter.2.cloned.1.call-done = bf16[32,4096]{1,0:T(8,128)(2,1)} async-done(((bf16[256,4096]{1,0:T(8,128)(2,1)}), bf16[32,4096]{1,0:T(8,128)(2,1)}) %reduce-scatter.2.cloned.1.call-update) | async-done | bytes 262160 | tf_op jit(solution)/shard_map/reduce_scatter | solution.py:222
  (114 shorter events, 12.7 us)
Async XLA Ops:
  7.2 72.4 %copy-start = (bf16[4096,128]{1,0:T(8,128)(2,1)S(1)}, bf16[4096,128]{1,0:T(8,128)(2,1)}, u32[]{:S(2)}) copy-start(bf16[4096,128]{1,0:T(8,128)(2,1)} %param.23) | copy-start | bytes 3145732
  7.2 34.2 %all-gather.4.cloned.1.call-start = ((), (), s32[]{:S(2)}) async-start(), calls=%async_computation.1 | async-start | bytes 2359296 | tf_op jit(solution)/shard_map/all_gather | solution.py:146
  10.2 111.4 %all-gather.6.cloned.1.call-start = ((), (), s32[]{:S(2)}) async-start(), calls=%async_computation.2 | async-start | bytes 4325376 | tf_op jit(solution)/shard_map/all_gather | solution.py:198
  11.0 191.8 %all-gather.8.cloned.1.call-start = ((), (), s32[]{:S(2)}) async-start(), calls=%async_computation.3 | async-start | bytes 4325376 | tf_op jit(solution)/shard_map/all_gather | solution.py:199
  11.7 256.9 %reduce-scatter.2.cloned.1.call-start = ((), (), s32[]{:S(2)}) async-start(), calls=%async_computation.4 | async-start | bytes 2359296 | tf_op jit(solution)/shard_map/reduce_scatter | solution.py:222
  46.1 0.9 copy-start.2
  46.1 0.9 copy-start.4
  47.0 32.6 %copy-start.1 = (bf16[256,4096]{1,0:T(8,128)(2,1)S(1)}, bf16[256,4096]{1,0:T(8,128)(2,1)}, u32[]{:S(2)}) copy-start(bf16[256,4096]{1,0:T(8,128)(2,1)} %all-gather.4.cloned.1.call-done) | copy-start | bytes 6291460
  79.6 7.7 %copy-start.11 = (f32[4,1,256]{2,1,0:T(1,128)}, f32[4,1,256]{2,1,0:T(1,128)S(1)}, u32[]{:S(2)}) copy-start(f32[4,1,256]{2,1,0:T(1,128)S(1)} %get-tuple-element.269) | copy-start | bytes 12292
  79.6 42.1 %copy-start.3 = (bf16[256,4,64]{2,1,0:T(4,128)(2,1)S(1)}, bf16[256,4,64]{2,1,0:T(4,128)(2,1)}, u32[]{:S(2)}) copy-start(bf16[256,4,64]{2,1,0:T(4,128)(2,1)} %copy-done.2) | copy-start | bytes 393220
  85.3 0.6 copy-start.7
  87.2 0.7 copy-start.5
  148.9 24.4 %copy-start.12 = (f32[4,1,256]{2,1,0:T(1,128)S(1)}, f32[4,1,256]{2,1,0:T(1,128)}, u32[]{:S(2)}) copy-start(f32[4,1,256]{2,1,0:T(1,128)} %copy-done.11) | copy-start | bytes 12292
  148.9 24.5 %copy-start.6 = (f32[4,256,64]{1,2,0:T(8,128)S(1)}, f32[4,256,64]{1,2,0:T(8,128)}, u32[]{:S(2)}) copy-start(f32[4,256,64]{1,2,0:T(8,128)} %copy-done.5) | copy-start | bytes 786436
  148.9 24.4 %copy-start.9 = (bf16[256,128]{1,0:T(8,128)(2,1)S(1)}, bf16[256,128]{1,0:T(8,128)(2,1)}, u32[]{:S(2)}) copy-start(bf16[256,128]{1,0:T(8,128)(2,1)} %convolution_convert_fusion.1) | copy-start | bytes 196612
  148.9 24.4 %copy-start.10 = (f32[4,1,256,128]{3,2,1,0:T(8,128)S(1)}, f32[4,1,256,128]{3,2,1,0:T(8,128)}, u32[]{:S(2)}) copy-start(f32[4,1,256,128]{3,2,1,0:T(8,128)} %get-tuple-element.268) | copy-start | bytes 1572868
  228.8 4.9 %copy-start.13 = (s32[4,8]{1,0:T(4,128)S(1)}, s32[4,8]{1,0:T(4,128)}, u32[]{:S(2)}) copy-start(s32[4,8]{1,0:T(4,128)} %param.33) | copy-start | bytes 388
  228.8 5.6 %copy-start.8 = (bf16[4,64,128]{2,1,0:T(8,128)(2,1)S(1)}, bf16[4,64,128]{2,1,0:T(8,128)(2,1)}, u32[]{:S(2)}) copy-start(bf16[4,64,128]{2,1,0:T(8,128)(2,1)} %copy-done.7) | copy-start | bytes 196612
Sparse Core Ops, SparseCore 0:
  10.4 30.8 all-gather.3
  43.9 77.6 all-gather.5
  124.2 78.4 all-gather.7
  233.8 34.7 reduce-scatter.1
where the time goes:
time: 280 us; the launch traced here: 275 us
  waiting for transfers between devices  117 us (42%)
  matrix products  80.3 us (29%)
  other arithmetic  35.3 us (13%)
  local copies, waits for them, and re-layouts  17.8 us (6%)
  between operations  14.2 us (5%)
  loops' own time  10.6 us (4%)
    reduce_scatter x1, waiting for transfers between devices, body(): lax.psum_scatter(jnp.dot(attended, w_out, preferred_element_type=jnp.floa...  32.8 us
    all_gather x1, waiting for transfers between devices, body(): piece_keys = lax.all_gather(prefix_keys, 'batch', axis=0, tiled=True)  31.1 us
    all_gather x1, waiting for transfers between devices, body(): piece_values = lax.all_gather(prefix_values, 'batch', axis=0, tiled=True)  28.4 us
    dot_general x1, matrix products, body(): jnp.einsum('rhqd,khd->rhqk', queries, shaped_keys, preferred_element_type...  27.2 us
    dot_general x1, matrix products, body(): jnp.einsum('rhqk,khd->rhqd', rounded, shaped_values, preferred_element_ty...  25.9 us
    reduce_sum x6, other arithmetic, absorb(): new_sum = running_sum * factor + jnp.sum(weights, axis=-1)  25 us
    all_gather x1, waiting for transfers between devices, body(): piece = lax.all_gather(normed, 'tensor', axis=0, tiled=True)  23.2 us
  transfers between devices with their start and end apart: 4, of which 4 were waited for; matrix products, arithmetic and copies ran while one was open for 36% of the time, Pallas kernels for 0%

commit v1 on v0

v1 whole, which is shorter than its diff:
```python
import jax
import jax.numpy as jnp
from jax import lax
from jax.experimental import pallas as pl
from jax.experimental.pallas import tpu as pltpu
from jax.sharding import PartitionSpec as P

HD = 128
TREE = 64
GROUP = 4
REQ = 4
NX = 4
NZ = 8
NY = 4
BLOCK = 512
CACHE_BLOCK = 512
NEG_FILL = -1e30
LOG2E = 1.4426950408889634
SCALE2 = HD ** (-0.5) * LOG2E
MESH = pl.DeviceIdType.MESH
ORDER = (0, 1, 3, 2)
F32 = jnp.float32
BF16 = jnp.bfloat16


def place():
    batch = lax.axis_index("batch")
    tensor = lax.axis_index("tensor")
    z, x = lax.div(batch, NX), lax.rem(batch, NX)
    y, core = lax.div(tensor, 2), lax.rem(tensor, 2)
    return batch, tensor, z, x, y, core


def remote(src, dst, send, recv, device):
    return pltpu.make_async_remote_copy(
        src_ref=src, dst_ref=dst, send_sem=send, recv_sem=recv, device_id=device, device_id_type=MESH
    )


def greet(devices):
    barrier = pltpu.get_barrier_semaphore()
    for device in devices:
        pl.semaphore_signal(barrier, inc=1, device_id=device, device_id_type=MESH)
    pl.semaphore_wait(barrier, len(devices))


def project_kernel(
    used_s, len_s, par, gain, freq, tok, wq, wk, wv, pk, pv,
    q_all, k_all, v_all, new_k, new_v, anc, used_all,
    tokb, wb, normb, qb, nkb, nvb, ancb, usedb, cosb, sinb, kvb,
    tok_s, tok_r, kv_s, kv_r, q_s, q_r, us_s, us_r, loc,
):
    batch, me, z, x, y, core = place()
    yp = lax.rem(y + 1, NY) * 2 + core
    ym = lax.rem(y + 3, NY) * 2 + core
    y2 = lax.rem(y + 2, NY) * 2 + core
    other = y * 2 + 1 - core
    oyp = lax.rem(y + 1, NY) * 2 + 1 - core
    oym = lax.rem(y + 3, NY) * 2 + 1 - core
    oy2 = lax.rem(y + 2, NY) * 2 + 1 - core
    zp = lax.rem(z + 1, NZ) * NX + x
    zm = lax.rem(z + NZ - 1, NZ) * NX + x
    x_up, x_down, x_far = lax.rem(x + 1, NX), lax.rem(x + 3, NX), lax.rem(x + 2, NX)
    xp, xm, xf = z * NX + x_up, z * NX + x_down, z * NX + x_far
    top, low = pl.ds(0, 16), pl.ds(16, 16)

    loads = [
        pltpu.make_async_copy(tok, tokb.at[me], loc.at[0]),
        pltpu.make_async_copy(wq, wb.at[:, pl.ds(0, 512)], loc.at[1]),
        pltpu.make_async_copy(wk, wb.at[:, pl.ds(512, 128)], loc.at[2]),
        pltpu.make_async_copy(wv, wb.at[:, pl.ds(640, 128)], loc.at[3]),
        pltpu.make_async_copy(pk, kvb.at[0], loc.at[4]),
        pltpu.make_async_copy(pv, kvb.at[1], loc.at[5]),
    ]
    for load in loads:
        load.start()

    lane = lax.broadcasted_iota(jnp.int32, (8, HD), 1)
    used_row = jnp.zeros((8, HD), jnp.int32)
    for r in range(REQ):
        used_row = jnp.where(lane == r, used_s[r], used_row)
    usedb[...] = used_row

    greet([(batch, yp), (batch, ym), (batch, other), (zp, me), (zm, me), (xp, me), (xm, me), (xf, me)])

    def tok_copy(index, src, slot, rows, target):
        dst = tokb.at[slot] if rows is None else tokb.at[slot, rows]
        return remote(src, dst, tok_s.at[index], tok_r.at[index], (batch, target))

    def tok_land(index, slot, rows):
        dst = tokb.at[slot] if rows is None else tokb.at[slot, rows]
        return remote(dst, dst, tok_s.at[index], tok_r.at[index], (batch, other))

    sends = []

    def go(copy):
        copy.start()
        sends.append(copy)

    def kv_parts(direction, chunk):
        hop = chunk // 2
        is_key = (chunk + direction) % 2 == 0
        gathered = k_all if is_key else v_all
        own = pk if is_key else pv
        return hop, gathered, own

    def kv_send(direction, chunk):
        hop, gathered, own = kv_parts(direction, chunk)
        if direction == 0:
            block, target = lax.rem(z + NZ - hop, NZ), zp
        else:
            block, target = lax.rem(z + hop, NZ), zm
        src = own if hop == 0 else gathered.at[block]
        go(remote(src, gathered.at[block], kv_s.at[direction, chunk], kv_r.at[direction, chunk], (target, me)))

    def kv_land(direction, chunk):
        hop, gathered, own = kv_parts(direction, chunk)
        if direction == 0:
            block = lax.rem(z + NZ - 1 - hop, NZ)
        else:
            block = lax.rem(z + 1 + hop, NZ)
        dst = gathered.at[block]
        remote(dst, dst, kv_s.at[direction, chunk], kv_r.at[direction, chunk], (zp, me)).wait_recv()

    def kv_step(chunk):
        for direction in range(2):
            kv_land(direction, chunk - 2)
            kv_send(direction, chunk)

    go(tok_copy(0, tok.at[top], me, top, yp))
    go(tok_copy(2, tok.at[low], me, low, ym))
    for direction in range(2):
        kv_send(direction, 0)
    go(tok_copy(4, tok, me, None, other))
    go(tok_copy(1, tok.at[low], me, low, yp))
    go(tok_copy(3, tok.at[top], me, top, ym))
    for direction in range(2):
        kv_send(direction, 1)
    for index, (target, device) in enumerate(((xp, x_up), (xm, x_down), (xf, x_far))):
        go(remote(usedb, used_all.at[x], us_s.at[index], us_r.at[index], (target, me)))

    row = lax.broadcasted_iota(jnp.int32, (TREE, TREE), 0)
    col = lax.broadcasted_iota(jnp.int32, (TREE, TREE), 1)
    tables = []
    for r in range(REQ):
        hit = (row == par[pl.ds(r, 1), :]) | (row == col)
        tables.append(jnp.where(hit, 1.0, 0.0))
    for repeat in range(6):
        tables = [
            jnp.minimum(jnp.dot(a.astype(BF16), a.astype(BF16), preferred_element_type=F32), 1.0) for a in tables
        ]
    upper = lax.broadcasted_iota(jnp.int32, (TREE, HD), 1) < HD // 2
    for r in range(REQ):
        table = tables[r].T
        ancb[pl.ds(r * TREE, TREE), :] = table
        depth = jnp.sum(table, axis=1, keepdims=True) - 1.0
        base = (used_s[r] + len_s[batch * REQ + r]).astype(F32)
        angles = (depth + base) * freq[...]
        cosb[r] = jnp.cos(angles)
        sine = jnp.sin(angles)
        sinb[r] = jnp.where(upper, -sine, sine)

    for load in loads:
        load.wait()
    stores = [
        pltpu.make_async_copy(kvb.at[0], k_all.at[z], loc.at[4]),
        pltpu.make_async_copy(kvb.at[1], v_all.at[z], loc.at[5]),
        pltpu.make_async_copy(usedb, used_all.at[x], loc.at[6]),
        pltpu.make_async_copy(ancb, anc, loc.at[7]),
    ]
    for store in stores:
        store.start()

    def request_of(j):
        return lax.rem(y + ORDER[j], NY)

    def project(j):
        r = request_of(j)
        for half in range(2):
            values = tokb[2 * r + half].astype(F32)
            factor = lax.rsqrt(jnp.mean(values * values, axis=-1, keepdims=True) + 1e-05)
            normb[pl.ds(half * 32, 32), :] = (values * factor * gain[...]).astype(BF16)

        def step(k, total):
            rows = pl.ds(pl.multiple_of(k * 512, 512), 512)
            return total + jnp.dot(normb[:, rows], wb[rows, :], preferred_element_type=F32)

        total = lax.fori_loop(0, 8, step, jnp.zeros((TREE, 768), F32))
        cosine, sine = cosb[r], sinb[r]

        def turn(head):
            return (head * cosine + pltpu.roll(head, HD // 2, 1) * sine).astype(BF16)

        for g in range(GROUP):
            qb[r, pl.ds(g * TREE, TREE), :] = turn(total[:, g * HD : (g + 1) * HD])
        nkb[r] = turn(total[:, 512:640])
        nvb[r] = total[:, 640:768].astype(BF16)
        go(remote(qb.at[r], q_all.at[x, r], q_s.at[0, j], q_r.at[0, j], (xp, me)))
        go(remote(qb.at[r], q_all.at[x, r], q_s.at[1, j], q_r.at[1, j], (xm, me)))

    def q_relay(j):
        r = request_of(j)
        lower = q_all.at[x_down, r]
        remote(lower, lower, q_s.at[0, j], q_r.at[0, j], (xp, me)).wait_recv()
        part = q_all.at[x_down, r, pl.ds(0, 128)]
        go(remote(part, part, q_s.at[2, j], q_r.at[2, j], (xp, me)))
        higher = q_all.at[x_up, r]
        remote(higher, higher, q_s.at[1, j], q_r.at[1, j], (xm, me)).wait_recv()
        part = q_all.at[x_up, r, pl.ds(128, 128)]
        go(remote(part, part, q_s.at[3, j], q_r.at[3, j], (xm, me)))

    tok_land(0, ym, top).wait_recv()
    go(tok_copy(5, tokb.at[ym, top], ym, top, yp))
    tok_land(2, yp, low).wait_recv()
    go(tok_copy(6, tokb.at[yp, low], yp, low, ym))
    kv_step(2)
    tok_land(4, other, None).wait_recv()
    project(0)
    tok_land(3, yp, top).wait_recv()
    go(tok_copy(8, tokb.at[yp], yp, None, other))
    tok_land(1, ym, low).wait_recv()
    go(tok_copy(7, tokb.at[ym], ym, None, other))
    kv_step(3)
    tok_land(8, oyp, None).wait_recv()
    project(1)
    q_relay(0)
    tok_land(5, y2, top).wait_recv()
    go(tok_copy(9, tokb.at[y2, top], y2, top, other))
    tok_land(6, y2, low).wait_recv()
    go(tok_copy(10, tokb.at[y2, low], y2, low, other))
    kv_step(4)
    tok_land(7, oym, None).wait_recv()
    project(2)
    q_relay(1)
    kv_step(5)
    tok_land(9, oy2, top).wait_recv()
    tok_land(10, oy2, low).wait_recv()
    project(3)
    out_copies = [
        pltpu.make_async_copy(qb, q_all.at[x], loc.at[0]),
        pltpu.make_async_copy(nkb, new_k, loc.at[1]),
        pltpu.make_async_copy(nvb, new_v, loc.at[2]),
    ]
    for copy in out_copies:
        copy.start()
    kv_step(6)
    q_relay(2)
    q_relay(3)
    for j in range(REQ):
        r = request_of(j)
        part = q_all.at[x_far, r, pl.ds(0, 128)]
        remote(part, part, q_s.at[2, j], q_r.at[2, j], (xp, me)).wait_recv()
        part = q_all.at[x_far, r, pl.ds(128, 128)]
        remote(part, part, q_s.at[3, j], q_r.at[3, j], (xm, me)).wait_recv()
    for index, device in enumerate((x_down, x_up, x_far)):
        dst = used_all.at[device]
        remote(dst, dst, us_s.at[index], us_r.at[index], (xp, me)).wait_recv()
    for chunk in (5, 6):
        for direction in range(2):
            kv_land(direction, chunk)
    for copy in stores + out_copies:
        copy.wait()
    for copy in sends:
        copy.wait_send()


def attend_kernel(
    used_s, len_s, idx_s, q_all, k_all, v_all, new_k, new_v, anc, cache_k, cache_v,
    o_part, stats, acc_k, acc_v,
    qv, kv, vv, nkv, nvv, ancv, ckv, cvv, mb, accb, ob, stb, stt, sem, out_sem,
):
    batch, me, z, x, y, core = place()
    loads = [
        pltpu.make_async_copy(q_all, qv, sem.at[0]),
        pltpu.make_async_copy(k_all, kv, sem.at[1]),
        pltpu.make_async_copy(v_all, vv.at[:, :, pl.ds(0, HD)], sem.at[2]),
        pltpu.make_async_copy(new_k, nkv, sem.at[3]),
        pltpu.make_async_copy(new_v, nvv.at[:, :, pl.ds(0, HD)], sem.at[4]),
        pltpu.make_async_copy(anc, ancv, sem.at[5]),
        pltpu.make_async_copy(cache_k, ckv, sem.at[6]),
        pltpu.make_async_copy(cache_v, cvv.at[:, pl.ds(0, HD)], sem.at[7]),
    ]
    for load in loads:
        load.start()
    vv[:, :, HD:] = jnp.ones((NZ, BLOCK, HD), BF16)
    nvv[:, :, HD:] = jnp.ones((REQ, TREE, HD), BF16)
    cvv[:, HD:] = jnp.ones((cvv.shape[0], HD), BF16)
    for load in loads[:3]:
        load.wait()

    def absorb(query, keys, values, mask):
        scores = lax.dot_general(query, keys, (((1,), (1,)), ((), ())), preferred_element_type=F32)
        if mask is not None:
            scores = jnp.where(mask(scores.shape), scores, NEG_FILL)
        old = mb[...]
        new = jnp.maximum(old, jnp.max(scores, axis=1, keepdims=True))
        weights = jnp.exp2((scores - new[:, :1]) * SCALE2).astype(BF16)
        factor = jnp.exp2((old - new) * SCALE2)
        mb[...] = new
        accb[...] = accb[...] * jnp.concatenate([factor, factor], axis=1) + jnp.dot(
            weights, values, preferred_element_type=F32
        )

    lane = lax.broadcasted_iota(jnp.int32, (256, HD), 1)

    def one_request(i, _):
        group = lax.div(i, REQ)
        r = lax.rem(i, REQ)
        peer = lax.rem(x + 1 + group, NX)
        query = qv[peer, r]
        used = used_s[peer, 0, r] - BLOCK * x
        full = lax.min(lax.div(used - BLOCK, BLOCK * NX) + 1, NZ)
        mb[...] = jnp.full((256, HD), NEG_FILL, F32)
        accb[...] = jnp.zeros((256, 2 * HD), F32)

        def block(b, _):
            absorb(query, kv[b], vv[b], None)
            return 0

        lax.fori_loop(0, full, block, 0)
        rest = used - full * (BLOCK * NX)

        @pl.when(jnp.logical_and(rest > 0, full < NZ))
        def _():
            absorb(query, kv[full], vv[full], lambda s: lax.broadcasted_iota(jnp.int32, s, 1) < rest)

        @pl.when(i == REQ * (NX - 1))
        def _():
            for load in loads[3:]:
                load.wait()

        @pl.when(group == NX - 1)
        def _():
            lower = lax.fori_loop(0, r, lambda p, t: t + len_s[batch * REQ + p], 0)
            upper = lower + len_s[batch * REQ + r]
            first = lax.div(lower, 16) * 16
            count = lax.div(upper - first + CACHE_BLOCK - 1, CACHE_BLOCK)

            def cache_step(b, _):
                begin = first + b * CACHE_BLOCK
                start = pl.multiple_of(lax.min(begin, cache_k.shape[0] - CACHE_BLOCK), 16)
                rows = pl.ds(start, CACHE_BLOCK)

                def mask(s):
                    slot = start + lax.broadcasted_iota(jnp.int32, s, 1)
                    return (slot >= lax.max(lower, begin)) & (slot < upper)

                absorb(query, ckv[rows, :], cvv[rows, :], mask)
                return 0

            lax.fori_loop(0, count, cache_step, 0)
            table = ancv[pl.ds(pl.multiple_of(r * TREE, TREE), TREE), :] > 0.5

            def tree_mask(s):
                tall = ancv[pl.ds(pl.multiple_of(r * TREE, TREE), TREE), :]
                return jnp.concatenate([tall] * GROUP, axis=0) > 0.5

            absorb(query, nkv[r], nvv[r], tree_mask)

        total = accb[...]
        ob[peer, r] = (total[:, :HD] / total[:, HD:]).astype(BF16)
        level = mb[...] * SCALE2 + jnp.log2(total[:, HD:])
        stb[...] = jnp.where(lane == r, level, stb[...])

        @pl.when(r == REQ - 1)
        def _():
            stt[peer] = stb[...].T[:8, :]

        return 0

    stb[...] = jnp.zeros((256, HD), F32)
    lax.fori_loop(0, REQ * NX, one_request, 0)
    outs = [
        pltpu.make_async_copy(ob, o_part, out_sem.at[0]),
        pltpu.make_async_copy(stt, stats, out_sem.at[1]),
    ]
    for out in outs:
        out.start()
    row = lax.broadcasted_iota(jnp.int32, (8, TREE), 0)
    col = lax.broadcasted_iota(jnp.int32, (8, TREE), 1)
    for r in range(REQ):
        pick = jnp.zeros((8, TREE), F32)
        for p in range(8):
            pick = jnp.where((row == p) & (col == idx_s[r, p]), 1.0, pick)
        pick = pick.astype(BF16)
        acc_k[r] = jnp.dot(pick, nkv[r], preferred_element_type=F32).astype(BF16)
        acc_v[r] = jnp.dot(pick, nvv[r, :, pl.ds(0, HD)], preferred_element_type=F32).astype(BF16)
    for out in outs:
        out.wait()


def mix_kernel(
    o_part, stats, w_out,
    out,
    wv, own, got, ownst, gotst, relay, att, pb, pr, sb, far, yb, yr,
    s_s, s_r, x_s, x_r, p_s, p_r, f_s, f_r, y_s, y_r, loc,
):
    batch, me, z, x, y, core = place()
    yup, ydown, yfar = lax.rem(y + 1, NY), lax.rem(y + 3, NY), lax.rem(y + 2, NY)
    yp, ym, other = yup * 2 + core, ydown * 2 + core, y * 2 + 1 - core
    x_up, x_down, x_far = lax.rem(x + 1, NX), lax.rem(x + 3, NX), lax.rem(x + 2, NX)
    xp, xm, xf = z * NX + x_up, z * NX + x_down, z * NX + x_far
    loads = [
        pltpu.make_async_copy(w_out, wv, loc.at[0]),
        pltpu.make_async_copy(o_part.at[x], own, loc.at[1]),
        pltpu.make_async_copy(stats.at[x], ownst, loc.at[2]),
    ]
    for load in loads:
        load.start()
    greet([(batch, yp), (batch, ym), (batch, other), (xp, me), (xm, me), (xf, me)])
    sends = []

    def go(copy):
        copy.start()
        sends.append(copy)

    turn = (yfar, yup, ydown, y)
    first, second = pl.ds(0, 128), pl.ds(128, 128)
    peers = ((x_up, xp), (x_down, xm), (x_far, xf))
    for index, (peer, target) in enumerate(peers):
        go(remote(stats.at[peer], gotst.at[index], s_s.at[index], s_r.at[index], (target, me)))

    for j in range(REQ):
        r = turn[j]
        go(remote(o_part.at[x_far, r, first], relay.at[0, j], x_s.at[0, j], x_r.at[0, j], (xp, me)))
        go(remote(o_part.at[x_far, r, second], relay.at[1, j], x_s.at[1, j], x_r.at[1, j], (xm, me)))
        go(remote(o_part.at[x_up, r], got.at[0, r], x_s.at[2, j], x_r.at[2, j], (xp, me)))
        go(remote(o_part.at[x_down, r], got.at[1, r], x_s.at[3, j], x_r.at[3, j], (xm, me)))

    def pass_on(j):
        r = turn[j]
        for side, (rows, target) in enumerate(((first, xp), (second, xm))):
            slot = relay.at[side, j]
            remote(slot, slot, x_s.at[side, j], x_r.at[side, j], (target, me)).wait_recv()
            go(remote(slot, got.at[2, r, rows], x_s.at[4 + side, j], x_r.at[4 + side, j], (target, me)))

    for load in loads:
        load.wait()
    for index in range(3):
        slot = gotst.at[index]
        remote(slot, slot, s_s.at[index], s_r.at[index], (xp, me)).wait_recv()
    pass_on(0)
    levels = [ownst[...]] + [gotst[index] for index in range(3)]
    most = levels[0]
    for level in levels[1:]:
        most = jnp.maximum(most, level)
    powers = [jnp.exp2(level - most) for level in levels]
    whole = powers[0] + powers[1] + powers[2] + powers[3]
    shares = [(power / whole).T for power in powers]
    lane = lax.broadcasted_iota(jnp.int32, (256, 8), 1)

    def blend(j):
        r = turn[j]
        for kind in (2, 3):
            slot = got.at[kind - 2, r]
            remote(slot, slot, x_s.at[kind, j], x_r.at[kind, j], (xp, me)).wait_recv()
        for kind, rows in ((4, first), (5, second)):
            slot = got.at[2, r, rows]
            remote(slot, slot, x_s.at[kind, j], x_r.at[kind, j], (xp, me)).wait_recv()
        total = jnp.zeros((256, HD), F32)
        for index in range(4):
            piece = own[r] if index == 0 else got[index - 1, r]
            share = jnp.sum(jnp.where(lane == r, shares[index], 0.0), axis=1, keepdims=True)
            total = total + share * piece.astype(F32)
        total = total.astype(BF16)
        for g in range(GROUP):
            att[:, pl.ds(g * HD, HD)] = total[g * TREE : (g + 1) * TREE, :]

        def columns(n, _):
            cols = pl.ds(pl.multiple_of(n * 1024, 1024), 1024)
            part = jnp.dot(att[...], wv[:, cols], preferred_element_type=F32).astype(BF16)
            pb[j, 0, :, cols] = part[:32, :]
            pb[j, 1, :, cols] = part[32:, :]
            return 0

        lax.fori_loop(0, 4, columns, 0)
        go(remote(pb.at[j, 1 - core], pr.at[j], p_s.at[j], p_r.at[j], (batch, other)))

    def pair_sum(j):
        slot = pr.at[j]
        remote(slot, slot, p_s.at[j], p_r.at[j], (batch, other)).wait_recv()
        return pb[j, core].astype(F32) + pr[j].astype(F32)

    top, low = pl.ds(0, 16), pl.ds(16, 16)
    blend(0)
    pass_on(1)
    blend(1)
    sb[...] = pair_sum(0).astype(BF16)
    go(remote(sb.at[top], far.at[0], f_s.at[0], f_r.at[0], (batch, yp)))
    go(remote(sb.at[low], far.at[1], f_s.at[1], f_r.at[1], (batch, ym)))
    pass_on(2)
    blend(2)
    slot = far.at[0]
    remote(slot, slot, f_s.at[0], f_r.at[0], (batch, yp)).wait_recv()
    value = pair_sum(1)
    yb[0, top, :] = (value[:16, :] + far[0].astype(F32)).astype(BF16)
    yb[0, low, :] = value[16:, :].astype(BF16)
    go(remote(yb.at[0], yr.at[0], y_s.at[0], y_r.at[0], (batch, yp)))
    pass_on(3)
    slot = far.at[1]
    remote(slot, slot, f_s.at[1], f_r.at[1], (batch, ym)).wait_recv()
    value = pair_sum(2)
    yb[1, top, :] = value[:16, :].astype(BF16)
    yb[1, low, :] = (value[16:, :] + far[1].astype(F32)).astype(BF16)
    go(remote(yb.at[1], yr.at[1], y_s.at[1], y_r.at[1], (batch, ym)))
    blend(3)
    value = pair_sum(3)
    for index in range(2):
        slot = yr.at[index]
        remote(slot, slot, y_s.at[index], y_r.at[index], (batch, yp)).wait_recv()
        value = value + yr[index].astype(F32)
    out[...] = value.astype(BF16)
    for copy in sends:
        copy.wait_send()


def body(
    tokens, norm_gain, w_query, w_key, w_value, w_out, prefix_keys, prefix_values,
    cache_keys, cache_values, cache_lengths, prefix_used, parents, accepted_index,
):
    exponents = -jnp.arange(HD // 2, dtype=F32) / (HD // 2)
    frequency = jnp.tile(10000.0 ** exponents, 2)[None, :]
    any_spec = pl.BlockSpec(memory_space=pl.ANY)
    smem = pl.BlockSpec(memory_space=pltpu.SMEM)
    vmem = pl.BlockSpec(memory_space=pltpu.VMEM)
    dma = pltpu.SemaphoreType.DMA
    shape = jax.ShapeDtypeStruct
    limit = 60 * 1024 * 1024
    q_all, k_all, v_all, new_k, new_v, anc, used_all = pl.pallas_call(
        project_kernel,
        out_shape=(
            shape((NX, REQ, 256, HD), BF16),
            shape((NZ, BLOCK, HD), BF16),
            shape((NZ, BLOCK, HD), BF16),
            shape((REQ, TREE, HD), BF16),
            shape((REQ, TREE, HD), BF16),
            shape((REQ * TREE, TREE), F32),
            shape((NX, 8, HD), jnp.int32),
        ),
        in_specs=[smem, smem, vmem, vmem, vmem] + [any_spec] * 6,
        out_specs=[any_spec] * 7,
        scratch_shapes=[
            pltpu.VMEM((8, 32, 4096), BF16),
            pltpu.VMEM((4096, 768), BF16),
            pltpu.VMEM((TREE, 4096), BF16),
            pltpu.VMEM((REQ, 256, HD), BF16),
            pltpu.VMEM((REQ, TREE, HD), BF16),
            pltpu.VMEM((REQ, TREE, HD), BF16),
            pltpu.VMEM((REQ * TREE, TREE), F32),
            pltpu.VMEM((8, HD), jnp.int32),
            pltpu.VMEM((REQ, TREE, HD), F32),
            pltpu.VMEM((REQ, TREE, HD), F32),
            pltpu.VMEM((2, BLOCK, HD), BF16),
            dma((11,)), dma((11,)), dma((2, 7)), dma((2, 7)), dma((4, REQ)), dma((4, REQ)), dma((3,)), dma((3,)),
            dma((8,)),
        ],
        compiler_params=pltpu.CompilerParams(collective_id=0, has_side_effects=True, vmem_limit_bytes=limit),
        name="project_and_gather",
    )(
        prefix_used, cache_lengths, parents, norm_gain[None, :], frequency, tokens, w_query, w_key, w_value,
        prefix_keys, prefix_values,
    )
    slots = cache_keys.shape[0]
    o_part, stats, acc_k, acc_v = pl.pallas_call(
        attend_kernel,
        out_shape=(
            shape((NX, REQ, 256, HD), BF16),
            shape((NX, 8, 256), F32),
            shape((REQ, 8, HD), BF16),
            shape((REQ, 8, HD), BF16),
        ),
        in_specs=[smem, smem, smem] + [any_spec] * 8,
        out_specs=[any_spec, any_spec, vmem, vmem],
        scratch_shapes=[
            pltpu.VMEM((NX, REQ, 256, HD), BF16),
            pltpu.VMEM((NZ, BLOCK, HD), BF16),
            pltpu.VMEM((NZ, BLOCK, 2 * HD), BF16),
            pltpu.VMEM((REQ, TREE, HD), BF16),
            pltpu.VMEM((REQ, TREE, 2 * HD), BF16),
            pltpu.VMEM((REQ * TREE, TREE), F32),
            pltpu.VMEM((slots, HD), BF16),
            pltpu.VMEM((slots, 2 * HD), BF16),
            pltpu.VMEM((256, HD), F32),
            pltpu.VMEM((256, 2 * HD), F32),
            pltpu.VMEM((NX, REQ, 256, HD), BF16),
            pltpu.VMEM((256, HD), F32),
            pltpu.VMEM((NX, 8, 256), F32),
            dma((8,)), dma((2,)),
        ],
        compiler_params=pltpu.CompilerParams(vmem_limit_bytes=limit),
        name="attend",
    )(
        used_all, cache_lengths, accepted_index, q_all, k_all, v_all, new_k, new_v, anc, cache_keys, cache_values
    )
    mixed = pl.pallas_call(
        mix_kernel,
        out_shape=shape((32, 4096), BF16),
        in_specs=[any_spec] * 3,
        out_specs=vmem,
        scratch_shapes=[
            pltpu.VMEM((512, 4096), BF16),
            pltpu.VMEM((REQ, 256, HD), BF16),
            pltpu.VMEM((3, REQ, 256, HD), BF16),
            pltpu.VMEM((8, 256), F32),
            pltpu.VMEM((3, 8, 256), F32),
            pltpu.VMEM((2, REQ, 128, HD), BF16),
            pltpu.VMEM((TREE, 512), BF16),
            pltpu.VMEM((REQ, 2, 32, 4096), BF16),
            pltpu.VMEM((REQ, 32, 4096), BF16),
            pltpu.VMEM((32, 4096), BF16),
            pltpu.VMEM((2, 16, 4096), BF16),
            pltpu.VMEM((2, 32, 4096), BF16),
            pltpu.VMEM((2, 32, 4096), BF16),
            dma((3,)), dma((3,)), dma((6, REQ)), dma((6, REQ)), dma((REQ,)), dma((REQ,)), dma((2,)), dma((2,)),
            dma((2,)), dma((2,)), dma((3,)),
        ],
        compiler_params=pltpu.CompilerParams(collective_id=1, has_side_effects=True, vmem_limit_bytes=limit),
        name="mix",
    )(o_part, stats, w_out)
    return (mixed, acc_k, acc_v)


def solution(mesh):
    in_specs = (
        P(("batch", "tensor"), None),
        P(),
        P(None, "tensor"),
        P(None, "tensor"),
        P(None, "tensor"),
        P("tensor", None),
        P("batch", "tensor"),
        P("batch", "tensor"),
        P("batch", "tensor"),
        P("batch", "tensor"),
        P(),
        P("batch"),
        P("batch", None),
        P("batch", None),
    )
    out_specs = (
        P(("batch", "tensor"), None),
        P("batch", None, "tensor"),
        P("batch", None, "tensor"),
    )
    return jax.shard_map(body, mesh=mesh, in_specs=in_specs, out_specs=out_specs, check_vma=False)
```

time: 280 us -> 156 us (0.56); the launches traced: 275 us -> 155 us
  Pallas kernels: 0 us -> 153 us
  waiting for transfers between devices: 117 us -> 0 us
  matrix products: 80.3 us -> 0 us
  other arithmetic: 35.3 us -> 0.01 us
  local copies, waits for them, and re-layouts: 17.8 us -> 2.26 us
  between operations: 14.2 us -> 0.67 us
  loops' own time: 10.6 us -> 0 us
    pallas_call x0 -> x3, Pallas kernels: none -> 153 us  [the longest x1 84.2 us: body(): pl.pallas_call(attend_kernel, out_shape=(shape((NX, REQ, 256, HD), BF16),...]
    all_gather x3 -> x0, waiting for transfers between devices: 82.6 us -> none  [the longest x1 31.1 us: body(): piece_keys = lax.all_gather(prefix_keys, 'batch', axis=0, tiled=True)]
    dot_general x23 -> x0, matrix products: 80.3 us -> none  [the longest x1 27.2 us: body(): jnp.einsum('rhqd,khd->rhqk', queries, shaped_keys, preferred_element_type...]
    reduce_scatter x1 -> x0, waiting for transfers between devices: 32.8 us -> none  [body(): lax.psum_scatter(jnp.dot(attended, w_out, preferred_element_type=jnp.floa...]
    reduce_sum x7 -> x0, other arithmetic: 26.2 us -> none  [the longest x6 25 us: absorb(): new_sum = running_sum * factor + jnp.sum(weights, axis=-1)]
    another operation x5 -> x0, loops' own time: 10.6 us -> none  [the longest x1 5.42 us: cache_partials(): return lax.map(one_request, (queries, lower_slot, upper_slot))]
    dynamic_slice x8 -> x0, local copies, waits for them, and re-layouts: 4.93 us -> none  [cache_partials(): return lax.map(one_request, (queries, lower_slot, upper_slot))]
    squeeze x4 -> x0, local copies, waits for them, and re-layouts: 3.4 us -> none  [cache_partials(): return lax.map(one_request, (queries, lower_slot, upper_slot))]
  transfers between devices with their start and end apart: 4 -> 0, of which waited for: 4 -> 0; matrix products, arithmetic and copies ran while one was open for 36% -> 0% of each run, Pallas kernels for 0% -> 0%
where the time goes in v1:
time: 156 us; the launch traced here: 155 us
  Pallas kernels  153 us (98%)
  local copies, waits for them, and re-layouts  2.26 us (1%)
    pallas_call x1, Pallas kernels, body(): pl.pallas_call(attend_kernel, out_shape=(shape((NX, REQ, 256, HD), BF16),...  84.2 us
    pallas_call x1, Pallas kernels, body(): pl.pallas_call(mix_kernel, out_shape=shape((32, 4096), BF16), in_specs=[a...  34.6 us
    pallas_call x1, Pallas kernels, body(): pl.pallas_call(project_kernel, out_shape=(shape((NX, REQ, 256, HD), BF16)...  33.7 us

profile of v1, /device:TPU:33, one launch (start us, length us, event | category | flops | bytes accessed | tf_op | source)
XLA Modules:
  0.0 155.4 jit_solution(1311466354487487199)
XLA Ops:
  0.7 0.6 broadcast_in_dim_tile.3.freq
  1.2 33.7 %project_and_gather.1 = (bf16[4,4,256,128]{3,2,1,0:T(8,128)(2,1)}, bf16[8,512,128]{2,1,0:T(8,128)(2,1)}, bf16[8,512,128]{2,1,0:T(8,128)(2,1)}, bf16[4,64,128]{2,...) custom-call(s32[4]{0:T(128)} %used_s.1, s32[128]{0:T(128)} %len_s.3, ...), custom_call_target="tpu_custom_call" | custom-call | tf_op jit(solution)/shard_map/project_and_gather/pallas_call | solution.py:529
  34.9 84.2 %attend.1 = (bf16[4,4,256,128]{3,2,1,0:T(8,128)(2,1)}, f32[4,8,256]{2,1,0:T(8,128)}, bf16[4,8,128]{2,1,0:T(8,128)(2,1)}, bf16[4,8,128]{2,1,0:T(8,128)(2,1)}) custom-call(s32[4,8,128]{2,1,0:T(8,128)} %get-tuple-element.14.used_s, s32[128]{0:T(128)} %len_s.3, s32[4,8]{1,0:T(4,128)} %idx_s.1, bf16[4,4,256,128]{3,2,1,0:T(8,128)(2,1)} %get-tuple-element.15.q_all, ...), custom_call_target="tpu_custom_call" | custom-call | tf_op jit(solution)/shard_map/attend/pallas_call | solution.py:564
  119.1 34.6 %mix.1 = bf16[32,4096]{1,0:T(8,128)(2,1)} custom-call(bf16[4,4,256,128]{3,2,1,0:T(8,128)(2,1)} %get-tuple-element.21.o_part, f32[4,8,256]{2,1,0:T(8,128)} %get-tuple-element.22.stats, bf16[512,4096]{1,0:T(8,128)(2,1)} %w_out.1), custom_call_target="tpu_custom_call" | custom-call | tf_op jit(solution)/shard_map/mix/pallas_call | solution.py:595
  153.8 1.7 %copy.18 = bf16[32,4096]{1,0:T(8,128)(2,1)} copy(bf16[32,4096]{1,0:T(8,128)(2,1)} %mix.1) | data formatting | bytes 524288
  (2 shorter events, 0.0 us)

commit v2 on v1

--- a/solution.py
+++ b/solution.py
@@ -13,7 +13,7 @@
 NZ = 8
 NY = 4
 BLOCK = 512
-CACHE_BLOCK = 512
+ITEMS = REQ * NX + REQ
 NEG_FILL = -1e30
 LOG2E = 1.4426950408889634
 SCALE2 = HD ** (-0.5) * LOG2E
@@ -152,7 +152,7 @@
     upper = lax.broadcasted_iota(jnp.int32, (TREE, HD), 1) < HD // 2
     for r in range(REQ):
         table = tables[r].T
-        ancb[pl.ds(r * TREE, TREE), :] = table
+        ancb[r] = jnp.concatenate([tables[r]] * GROUP, axis=1)
         depth = jnp.sum(table, axis=1, keepdims=True) - 1.0
         base = (used_s[r] + len_s[batch * REQ + r]).astype(F32)
         angles = (depth + base) * freq[...]
@@ -267,124 +267,167 @@
 def attend_kernel(
     used_s, len_s, idx_s, q_all, k_all, v_all, new_k, new_v, anc, cache_k, cache_v,
     o_part, stats, acc_k, acc_v,
-    qv, kv, vv, nkv, nvv, ancv, ckv, cvv, mb, accb, ob, stb, stt, sem, out_sem,
+    qv, kv, vb, vt, nkv, nvv, ancv, sc, mb, accb, ob, lv, stt, items, order, sem, out_sem,
 ):
     batch, me, z, x, y, core = place()
+    prefix_rows = NZ * BLOCK
+    slots = cache_k.shape[0]
     loads = [
-        pltpu.make_async_copy(q_all, qv, sem.at[0]),
-        pltpu.make_async_copy(k_all, kv, sem.at[1]),
-        pltpu.make_async_copy(v_all, vv.at[:, :, pl.ds(0, HD)], sem.at[2]),
-        pltpu.make_async_copy(new_k, nkv, sem.at[3]),
-        pltpu.make_async_copy(new_v, nvv.at[:, :, pl.ds(0, HD)], sem.at[4]),
-        pltpu.make_async_copy(anc, ancv, sem.at[5]),
-        pltpu.make_async_copy(cache_k, ckv, sem.at[6]),
-        pltpu.make_async_copy(cache_v, cvv.at[:, pl.ds(0, HD)], sem.at[7]),
+        pltpu.make_async_copy(v_all, vb.at[pl.ds(0, prefix_rows)], sem.at[0]),
+        pltpu.make_async_copy(cache_v, vb.at[pl.ds(prefix_rows, slots)], sem.at[1]),
+        pltpu.make_async_copy(k_all, kv.at[pl.ds(0, prefix_rows)], sem.at[2]),
+        pltpu.make_async_copy(cache_k, kv.at[pl.ds(prefix_rows, slots)], sem.at[3]),
+        pltpu.make_async_copy(q_all, qv, sem.at[4]),
+        pltpu.make_async_copy(new_k, nkv, sem.at[5]),
+        pltpu.make_async_copy(new_v, nvv, sem.at[6]),
+        pltpu.make_async_copy(anc, ancv, sem.at[7]),
     ]
     for load in loads:
         load.start()
-    vv[:, :, HD:] = jnp.ones((NZ, BLOCK, HD), BF16)
-    nvv[:, :, HD:] = jnp.ones((REQ, TREE, HD), BF16)
-    cvv[:, HD:] = jnp.ones((cvv.shape[0], HD), BF16)
-    for load in loads[:3]:
+
+    def note(i, blocks, query, first, lower, upper):
+        for field, value in enumerate((blocks, query, first, lower, upper)):
+            items[field, i] = value
+
+    def prefix_item(i, _):
+        used = used_s[lax.div(i, REQ), 0, lax.rem(i, REQ)] - BLOCK * x
+        full = lax.min(lax.div(used - BLOCK, BLOCK * NX) + 1, NZ)
+        rest = jnp.where(full < NZ, lax.max(used - full * (BLOCK * NX), 0), 0)
+        note(i, full + jnp.where(rest > 0, 1, 0), i, 0, 0, full * BLOCK + rest)
+        return 0
+
+    def cache_item(r, lower):
+        upper = lower + len_s[batch * REQ + r]
+        first = lax.div(lower, 128) * 128
+        blocks = lax.div(upper - first + BLOCK - 1, BLOCK)
+        first = lax.min(first, slots - blocks * BLOCK)
+        note(REQ * NX + r, blocks, x * REQ + r, prefix_rows + first, lower - first, upper - first)
+        return upper
+
+    lax.fori_loop(0, REQ * NX, prefix_item, 0)
+    lax.fori_loop(0, REQ, cache_item, 0)
+
+    def by_size(v, spot):
+        def put(i, spot):
+            order[spot] = i
+            return spot + jnp.where(items[0, i] == NZ - v, 1, 0)
+
+        return lax.fori_loop(0, ITEMS, put, spot)
+
+    lax.fori_loop(0, NZ, by_size, 0)
+
+    vt[HD:, :] = jnp.ones((16, vt.shape[1]), BF16)
+    loads[0].wait()
+    for n in range(NZ):
+        vt[:HD, n * BLOCK : (n + 1) * BLOCK] = vb[n * BLOCK : (n + 1) * BLOCK, :].T
+    loads[1].wait()
+    for n in range(NZ, (prefix_rows + slots) // BLOCK):
+        vt[:HD, n * BLOCK : (n + 1) * BLOCK] = vb[n * BLOCK : (n + 1) * BLOCK, :].T
+    for load in loads[2:]:
         load.wait()
 
-    def absorb(query, keys, values, mask):
-        scores = lax.dot_general(query, keys, (((1,), (1,)), ((), ())), preferred_element_type=F32)
-        if mask is not None:
-            scores = jnp.where(mask(scores.shape), scores, NEG_FILL)
-        old = mb[...]
-        new = jnp.maximum(old, jnp.max(scores, axis=1, keepdims=True))
-        weights = jnp.exp2((scores - new[:, :1]) * SCALE2).astype(BF16)
-        factor = jnp.exp2((old - new) * SCALE2)
-        mb[...] = new
-        accb[...] = accb[...] * jnp.concatenate([factor, factor], axis=1) + jnp.dot(
-            weights, values, preferred_element_type=F32
-        )
-
-    lane = lax.broadcasted_iota(jnp.int32, (256, HD), 1)
-
-    def one_request(i, _):
-        group = lax.div(i, REQ)
-        r = lax.rem(i, REQ)
-        peer = lax.rem(x + 1 + group, NX)
-        query = qv[peer, r]
-        used = used_s[peer, 0, r] - BLOCK * x
-        full = lax.min(lax.div(used - BLOCK, BLOCK * NX) + 1, NZ)
-        mb[...] = jnp.full((256, HD), NEG_FILL, F32)
-        accb[...] = jnp.zeros((256, 2 * HD), F32)
-
-        def block(b, _):
-            absorb(query, kv[b], vv[b], None)
-            return 0
-
-        lax.fori_loop(0, full, block, 0)
-        rest = used - full * (BLOCK * NX)
-
-        @pl.when(jnp.logical_and(rest > 0, full < NZ))
+    def dot_last(a, b):
+        return lax.dot_general(a, b, (((1,), (1,)), ((), ())), preferred_element_type=F32)
+
+    def fold(values, op):
+        while values.shape[0] > 8:
+            half = values.shape[0] // 2
+            values = op(values[:half], values[half:])
+        return values
+
+    row = lax.broadcasted_iota(jnp.int32, (BLOCK, HD), 0)
+
+    def score(item, slot, b):
+        rows = pl.ds(pl.multiple_of(items[2, item] + b * BLOCK, 128), BLOCK)
+        values = dot_last(kv[rows, :], qv[items[1, item]])
+        place_row = row + b * BLOCK
+        seen = (place_row >= items[3, item]) & (place_row < items[4, item])
+        for side in range(2):
+            lanes = slice(side * HD, (side + 1) * HD)
+            part = jnp.where(seen, values[:, lanes], NEG_FILL)
+            sc[slot, pl.ds(b * BLOCK, BLOCK), lanes] = part
+            best = part[:64]
+            for j in range(1, BLOCK // 64):
+                best = jnp.maximum(best, part[j * 64 : (j + 1) * 64])
+            mb[slot, :, lanes] = jnp.maximum(mb[slot, :, lanes], fold(best, jnp.maximum))
+
+    def gather_values(item, slot, b):
+        cols = pl.ds(pl.multiple_of(items[2, item] + b * BLOCK, 128), BLOCK)
+        weights = jnp.exp2((sc[slot, pl.ds(b * BLOCK, BLOCK), :] - mb[slot, :1, :]) * SCALE2).astype(BF16)
+        return jnp.dot(vt[:, cols], weights, preferred_element_type=F32)
+
+    def clear(slot):
+        mb[slot] = jnp.full((8, 256), NEG_FILL, F32)
+
+    clear(0)
+    lead = order[0]
+    for b in range(NZ):
+
+        @pl.when(b < items[0, lead])
         def _():
-            absorb(query, kv[full], vv[full], lambda s: lax.broadcasted_iota(jnp.int32, s, 1) < rest)
-
-        @pl.when(i == REQ * (NX - 1))
-        def _():
-            for load in loads[3:]:
-                load.wait()
-
-        @pl.when(group == NX - 1)
-        def _():
-            lower = lax.fori_loop(0, r, lambda p, t: t + len_s[batch * REQ + p], 0)
-            upper = lower + len_s[batch * REQ + r]
-            first = lax.div(lower, 16) * 16
-            count = lax.div(upper - first + CACHE_BLOCK - 1, CACHE_BLOCK)
-
-            def cache_step(b, _):
-                begin = first + b * CACHE_BLOCK
-                start = pl.multiple_of(lax.min(begin, cache_k.shape[0] - CACHE_BLOCK), 16)
-                rows = pl.ds(start, CACHE_BLOCK)
-
-                def mask(s):
-                    slot = start + lax.broadcasted_iota(jnp.int32, s, 1)
-                    return (slot >= lax.max(lower, begin)) & (slot < upper)
-
-                absorb(query, ckv[rows, :], cvv[rows, :], mask)
-                return 0
-
-            lax.fori_loop(0, count, cache_step, 0)
-            table = ancv[pl.ds(pl.multiple_of(r * TREE, TREE), TREE), :] > 0.5
-
-            def tree_mask(s):
-                tall = ancv[pl.ds(pl.multiple_of(r * TREE, TREE), TREE), :]
-                return jnp.concatenate([tall] * GROUP, axis=0) > 0.5
-
-            absorb(query, nkv[r], nvv[r], tree_mask)
-
-        total = accb[...]
-        ob[peer, r] = (total[:, :HD] / total[:, HD:]).astype(BF16)
-        level = mb[...] * SCALE2 + jnp.log2(total[:, HD:])
-        stb[...] = jnp.where(lane == r, level, stb[...])
-
-        @pl.when(r == REQ - 1)
-        def _():
-            stt[peer] = stb[...].T[:8, :]
-
+            score(lead, 0, b)
+
+    def pair(h, _):
+        for slot in range(2):
+            item = order[2 * h + slot]
+            after = order[lax.min(2 * h + slot + 1, ITEMS - 1)]
+            mb[slot] = jnp.broadcast_to(jnp.max(mb[slot], axis=0, keepdims=True), (8, 256))
+            clear(1 - slot)
+            for size in range(1, NZ + 1):
+
+                @pl.when(items[0, item] == size)
+                def _():
+                    total = None
+                    for b in range(size):
+                        part = gather_values(item, slot, b)
+                        total = part if total is None else total + part
+                        score(after, 1 - slot, b)
+                    accb[...] = total
+
+            mass = accb[HD : HD + 1, :]
+            ob[item] = (accb[:HD, :] / mass).astype(BF16)
+            lv[item] = jnp.broadcast_to(mb[slot, :1, :] * SCALE2 + jnp.log2(mass), (8, 256))
         return 0
 
-    stb[...] = jnp.zeros((256, HD), F32)
-    lax.fori_loop(0, REQ * NX, one_request, 0)
+    lax.fori_loop(0, ITEMS // 2, pair, 0)
+
+    for r in range(REQ):
+        values = dot_last(nkv[r], qv[x * REQ + r])
+        values = jnp.where(ancv[r] > 0.5, values, NEG_FILL)
+        best = jnp.max(values, axis=0, keepdims=True)
+        weights = jnp.exp2((values - best) * SCALE2)
+        mass = jnp.sum(weights, axis=0, keepdims=True)
+        tree_out = jnp.dot(nvv[r].T, weights.astype(BF16), preferred_element_type=F32) / mass
+        levels = (best * SCALE2 + jnp.log2(mass), lv[x * REQ + r, :1, :], lv[REQ * NX + r, :1, :])
+        top = jnp.maximum(jnp.maximum(levels[0], levels[1]), levels[2])
+        shares = [jnp.exp2(level - top) for level in levels]
+        whole = shares[0] + shares[1] + shares[2]
+        merged = (
+            shares[0] * tree_out
+            + shares[1] * ob[x * REQ + r].astype(F32)
+            + shares[2] * ob[REQ * NX + r].astype(F32)
+        ) / whole
+        ob[x * REQ + r] = merged.astype(BF16)
+        lv[x * REQ + r] = jnp.broadcast_to(top + jnp.log2(whole), (8, 256))
+    for peer in range(NX):
+        for r in range(REQ):
+            stt[peer, r : r + 1, :] = lv[peer * REQ + r, :1, :]
+            stt[peer, REQ + r : REQ + r + 1, :] = lv[peer * REQ + r, :1, :]
     outs = [
-        pltpu.make_async_copy(ob, o_part, out_sem.at[0]),
+        pltpu.make_async_copy(ob.at[pl.ds(0, REQ * NX)], o_part, out_sem.at[0]),
         pltpu.make_async_copy(stt, stats, out_sem.at[1]),
     ]
     for out in outs:
         out.start()
-    row = lax.broadcasted_iota(jnp.int32, (8, TREE), 0)
-    col = lax.broadcasted_iota(jnp.int32, (8, TREE), 1)
+    row8 = lax.broadcasted_iota(jnp.int32, (8, TREE), 0)
+    col8 = lax.broadcasted_iota(jnp.int32, (8, TREE), 1)
     for r in range(REQ):
         pick = jnp.zeros((8, TREE), F32)
         for p in range(8):
-            pick = jnp.where((row == p) & (col == idx_s[r, p]), 1.0, pick)
+            pick = jnp.where((row8 == p) & (col8 == idx_s[r, p]), 1.0, pick)
         pick = pick.astype(BF16)
         acc_k[r] = jnp.dot(pick, nkv[r], preferred_element_type=F32).astype(BF16)
-        acc_v[r] = jnp.dot(pick, nvv[r, :, pl.ds(0, HD)], preferred_element_type=F32).astype(BF16)
+        acc_v[r] = jnp.dot(pick, nvv[r], preferred_element_type=F32).astype(BF16)
     for out in outs:
         out.wait()
 
@@ -392,7 +435,7 @@
 def mix_kernel(
     o_part, stats, w_out,
     out,
-    wv, own, got, ownst, gotst, relay, att, pb, pr, sb, far, yb, yr,
+    wv, own, got, ownst, gotst, shareb, relay, att, pb, pr, sb, far, yb, yr,
     s_s, s_r, x_s, x_r, p_s, p_r, f_s, f_r, y_s, y_r, loc,
 ):
     batch, me, z, x, y, core = place()
@@ -415,7 +458,7 @@
         sends.append(copy)
 
     turn = (yfar, yup, ydown, y)
-    first, second = pl.ds(0, 128), pl.ds(128, 128)
+    first, second = pl.ds(0, 64), pl.ds(64, 64)
     peers = ((x_up, xp), (x_down, xm), (x_far, xf))
     for index, (peer, target) in enumerate(peers):
         go(remote(stats.at[peer], gotst.at[index], s_s.at[index], s_r.at[index], (target, me)))
@@ -446,8 +489,8 @@
         most = jnp.maximum(most, level)
     powers = [jnp.exp2(level - most) for level in levels]
     whole = powers[0] + powers[1] + powers[2] + powers[3]
-    shares = [(power / whole).T for power in powers]
-    lane = lax.broadcasted_iota(jnp.int32, (256, 8), 1)
+    for index in range(4):
+        shareb[index] = powers[index] / whole
 
     def blend(j):
         r = turn[j]
@@ -457,12 +500,11 @@
         for kind, rows in ((4, first), (5, second)):
             slot = got.at[2, r, rows]
             remote(slot, slot, x_s.at[kind, j], x_r.at[kind, j], (xp, me)).wait_recv()
-        total = jnp.zeros((256, HD), F32)
+        total = jnp.zeros((HD, 256), F32)
         for index in range(4):
             piece = own[r] if index == 0 else got[index - 1, r]
-            share = jnp.sum(jnp.where(lane == r, shares[index], 0.0), axis=1, keepdims=True)
-            total = total + share * piece.astype(F32)
-        total = total.astype(BF16)
+            total = total + shareb[index, pl.ds(r, 1), :] * piece.astype(F32)
+        total = total.T.astype(BF16)
         for g in range(GROUP):
             att[:, pl.ds(g * HD, HD)] = total[g * TREE : (g + 1) * TREE, :]
 
@@ -534,7 +576,7 @@
             shape((NZ, BLOCK, HD), BF16),
             shape((REQ, TREE, HD), BF16),
             shape((REQ, TREE, HD), BF16),
-            shape((REQ * TREE, TREE), F32),
+            shape((REQ, TREE, 256), F32),
             shape((NX, 8, HD), jnp.int32),
         ),
         in_specs=[smem, smem, vmem, vmem, vmem] + [any_spec] * 6,
@@ -546,7 +588,7 @@
             pltpu.VMEM((REQ, 256, HD), BF16),
             pltpu.VMEM((REQ, TREE, HD), BF16),
             pltpu.VMEM((REQ, TREE, HD), BF16),
-            pltpu.VMEM((REQ * TREE, TREE), F32),
+            pltpu.VMEM((REQ, TREE, 256), F32),
             pltpu.VMEM((8, HD), jnp.int32),
             pltpu.VMEM((REQ, TREE, HD), F32),
             pltpu.VMEM((REQ, TREE, HD), F32),
@@ -561,10 +603,11 @@
         prefix_keys, prefix_values,
     )
     slots = cache_keys.shape[0]
+    rows = NZ * BLOCK + slots
     o_part, stats, acc_k, acc_v = pl.pallas_call(
         attend_kernel,
         out_shape=(
-            shape((NX, REQ, 256, HD), BF16),
+            shape((NX * REQ, HD, 256), BF16),
             shape((NX, 8, 256), F32),
             shape((REQ, 8, HD), BF16),
             shape((REQ, 8, HD), BF16),
@@ -572,26 +615,30 @@
         in_specs=[smem, smem, smem] + [any_spec] * 8,
         out_specs=[any_spec, any_spec, vmem, vmem],
         scratch_shapes=[
-            pltpu.VMEM((NX, REQ, 256, HD), BF16),
-            pltpu.VMEM((NZ, BLOCK, HD), BF16),
-            pltpu.VMEM((NZ, BLOCK, 2 * HD), BF16),
+            pltpu.VMEM((NX * REQ, 256, HD), BF16),
+            pltpu.VMEM((rows + NZ * BLOCK, HD), BF16),
+            pltpu.VMEM((rows, HD), BF16),
+            pltpu.VMEM((HD + 16, rows), BF16),
             pltpu.VMEM((REQ, TREE, HD), BF16),
-            pltpu.VMEM((REQ, TREE, 2 * HD), BF16),
-            pltpu.VMEM((REQ * TREE, TREE), F32),
-            pltpu.VMEM((slots, HD), BF16),
-            pltpu.VMEM((slots, 2 * HD), BF16),
-            pltpu.VMEM((256, HD), F32),
-            pltpu.VMEM((256, 2 * HD), F32),
-            pltpu.VMEM((NX, REQ, 256, HD), BF16),
-            pltpu.VMEM((256, HD), F32),
+            pltpu.VMEM((REQ, TREE, HD), BF16),
+            pltpu.VMEM((REQ, TREE, 256), F32),
+            pltpu.VMEM((2, NZ * BLOCK, 256), F32),
+            pltpu.VMEM((2, 8, 256), F32),
+            pltpu.VMEM((HD + 16, 256), F32),
+            pltpu.VMEM((ITEMS, HD, 256), BF16),
+            pltpu.VMEM((ITEMS, 8, 256), F32),
             pltpu.VMEM((NX, 8, 256), F32),
+            pltpu.SMEM((5, ITEMS), jnp.int32),
+            pltpu.SMEM((ITEMS + 1,), jnp.int32),
             dma((8,)), dma((2,)),
         ],
         compiler_params=pltpu.CompilerParams(vmem_limit_bytes=limit),
         name="attend",
     )(
-        used_all, cache_lengths, accepted_index, q_all, k_all, v_all, new_k, new_v, anc, cache_keys, cache_values
+        used_all, cache_lengths, accepted_index, q_all.reshape(NX * REQ, 256, HD), k_all.reshape(-1, HD),
+        v_all.reshape(-1, HD), new_k, new_v, anc, cache_keys, cache_values,
     )
+    o_part = o_part.reshape(NX, REQ, HD, 256)
     mixed = pl.pallas_call(
         mix_kernel,
         out_shape=shape((32, 4096), BF16),
@@ -599,11 +646,12 @@
         out_specs=vmem,
         scratch_shapes=[
             pltpu.VMEM((512, 4096), BF16),
-            pltpu.VMEM((REQ, 256, HD), BF16),
-            pltpu.VMEM((3, REQ, 256, HD), BF16),
+            pltpu.VMEM((REQ, HD, 256), BF16),
+            pltpu.VMEM((3, REQ, HD, 256), BF16),
             pltpu.VMEM((8, 256), F32),
             pltpu.VMEM((3, 8, 256), F32),
-            pltpu.VMEM((2, REQ, 128, HD), BF16),
+            pltpu.VMEM((4, 8, 256), F32),
+            pltpu.VMEM((2, REQ, HD // 2, 256), BF16),
             pltpu.VMEM((TREE, 512), BF16),
             pltpu.VMEM((REQ, 2, 32, 4096), BF16),
             pltpu.VMEM((REQ, 32, 4096), BF16),

time: 156 us -> 99.6 us (0.64)
  the two profiles are of different devices: /device:TPU:33 before, /device:TPU:1 now
where the time goes in v2:
time: 99.6 us; the launch traced here: 98.7 us
  Pallas kernels  95.7 us (96%)
  local copies, waits for them, and re-layouts  2.26 us (2%)
    pallas_call x1, Pallas kernels, body(): pl.pallas_call(project_kernel, out_shape=(shape((NX, REQ, 256, HD), BF16)...  36.7 us
    pallas_call x1, Pallas kernels, body(): pl.pallas_call(mix_kernel, out_shape=shape((32, 4096), BF16), in_specs=[a...  33.6 us
    pallas_call x1, Pallas kernels, body(): pl.pallas_call(attend_kernel, out_shape=(shape((NX * REQ, HD, 256), BF16)...  25.5 us

profile of v2, /device:TPU:1, one launch (start us, length us, event | category | flops | bytes accessed | tf_op | source)
XLA Modules:
  0.0 98.7 jit_solution(15856741108381082321)
XLA Ops:
  0.7 0.6 broadcast_in_dim_tile.3.freq
  1.2 36.7 %project_and_gather.1 = (bf16[4,4,256,128]{3,2,1,0:T(8,128)(2,1)}, bf16[8,512,128]{2,1,0:T(8,128)(2,1)}, bf16[8,512,128]{2,1,0:T(8,128)(2,1)}, bf16[4,64,128]{2,...) custom-call(s32[4]{0:T(128)} %used_s.1, s32[128]{0:T(128)} %len_s.3, ...), custom_call_target="tpu_custom_call" | custom-call | tf_op jit(solution)/shard_map/project_and_gather/pallas_call | solution.py:571
  38.0 25.5 %attend.1 = (bf16[16,128,256]{2,1,0:T(8,128)(2,1)}, f32[4,8,256]{2,1,0:T(8,128)}, bf16[4,8,128]{2,1,0:T(8,128)(2,1)}, bf16[4,8,128]{2,1,0:T(8,128)(2,1)}) custom-call(s32[4,8,128]{2,1,0:T(8,128)} %get-tuple-element.14.used_s, s32[128]{0:T(128)} %len_s.3, s32[4,8]{1,0:T(4,128)} %idx_s.1, bf16[16,256,128]{2,1,0:T(8,128)(2,1)} %bitcast.5, ...), custom_call_target="tpu_custom_call" | custom-call | tf_op jit(solution)/shard_map/attend/pallas_call | solution.py:607
  63.4 33.6 %mix.1 = bf16[32,4096]{1,0:T(8,128)(2,1)} custom-call(bf16[4,4,128,256]{3,2,1,0:T(8,128)(2,1)} %bitcast.8, f32[4,8,256]{2,1,0:T(8,128)} %get-tuple-element.22.stats, bf16[512,4096]{1,0:T(8,128)(2,1)} %w_out.1), custom_call_target="tpu_custom_call" | custom-call | tf_op jit(solution)/shard_map/mix/pallas_call | solution.py:642
  97.0 1.7 %copy.18 = bf16[32,4096]{1,0:T(8,128)(2,1)} copy(bf16[32,4096]{1,0:T(8,128)(2,1)} %mix.1) | data formatting | bytes 524288
  (2 shorter events, 0.0 us)
